TPU v7x, 512 devices: a whole 4x8x8 slice. The times are simulated.
512 devices in a mesh: grp: 16 (over y, core), mdl: 32 (over x, z).
Axes of the slice: x: 4, y: 8, z: 8, core: 2. Of those that a mesh axis runs over, the one named last changes fastest.
Arguments:
- row_states: bfloat16 [6144, 1024], P('grp', 'mdl'), may hold values from -6 to 6
- ffn_gain: bfloat16 [1024], replicated, may hold values from 0.25 to 1.75
- ffn_in: bfloat16 [1024, 32768], P('grp', 'mdl'), may hold values from -0.1875 to 0.1875
- ffn_out: bfloat16 [32768, 1024], P('mdl', 'grp'), may hold values from -0.0625 to 0.0625
- final_gain: bfloat16 [1024], replicated, may hold values from 0.25 to 1.75
- kv_weight: bfloat16 [2, 1024, 16384], P(None, None, 'mdl'), may hold values from -0.1875 to 0.1875
- queries: bfloat16 [4096, 16384], P('grp', 'mdl'), may hold values from -36 to 36
- attn_out: bfloat16 [16384, 1024], P('mdl'), may hold values from -0.75 to 0.75
- row_question: int32 [6144], replicated, may hold values from 0 to 15, as said below
Outputs:
- cross_out: bfloat16 [4096, 1024], P(('grp', 'mdl'))
Inputs may be any that keep to these rules, and one draw needn't show every extreme that they name: `row_question`: within each block of 384 rows (one row group) the rows are sorted by question; in every block each question owns a multiple of 8 rows, at least 8 and at most 72, and one question, drawn from the seed, owns exactly 72 rows of every block.
All inputs are finite; a program needn't handle non-finite values.
Results may differ from a plain program's by a relative error of at most 0.029.
Values may be sent and summed in bfloat16 or wider, within the bound.
No kernel may reach another device: no remote copies, remote signals or barrier semaphores. Data moves between devices by JAX's collectives and lax.ppermute only.
A program may use at most 64 MiB of HBM per device.

v0:
```python
import jax
import jax.numpy as jnp
from jax import lax
from jax.sharding import PartitionSpec as P

HEAD_DIM = 128


def rms_normalize(states, gain):
    wide = states.astype(jnp.float32)
    factor = lax.rsqrt(jnp.mean(wide * wide, axis=-1, keepdims=True) + 1e-06)
    return (wide * factor * gain.astype(jnp.float32)).astype(jnp.bfloat16)


def bucket_plan(row_question, rows_local, groups, my_group):
    capacity = 3 * rows_local // groups
    owners = row_question.reshape(groups, rows_local)
    owner_table = (owners[:, :, None] == jnp.arange(groups, dtype=jnp.int32)[None, None, :]).astype(
        jnp.int32
    )
    counts = jnp.sum(owner_table, axis=1)
    starts = jnp.cumsum(counts, axis=1) - counts
    slot_index = jnp.arange(capacity, dtype=jnp.int32)
    sent_counts = lax.dynamic_index_in_dim(counts, my_group, 0, keepdims=False)
    sent_starts = lax.dynamic_index_in_dim(starts, my_group, 0, keepdims=False)
    send_valid = slot_index[None, :] < sent_counts[:, None]
    send_rows = jnp.minimum(sent_starts[:, None] + slot_index[None, :], rows_local - 1)
    got_counts = lax.dynamic_index_in_dim(counts, my_group, 1, keepdims=False)
    got_valid = (slot_index[None, :] < got_counts[:, None]).reshape(-1)
    return (capacity, send_rows, send_valid, got_valid)


def pack_slots(source, send_rows, send_valid):
    picked = jnp.take(source, send_rows.reshape(-1), axis=0)
    picked = picked.reshape(send_rows.shape[0], send_rows.shape[1], source.shape[1])
    picked = jnp.where(send_valid[:, :, None], picked, jnp.zeros((), source.dtype))
    return picked.reshape(send_rows.shape[0], -1)


def local(
    row_states, ffn_gain, ffn_in, ffn_out, final_gain, kv_weight, queries, attn_out, row_question
):
    groups = lax.axis_size("grp")
    my_group = lax.axis_index("grp")
    rows_local = row_states.shape[0]
    full_rows = lax.all_gather(row_states, "mdl", axis=1, tiled=True)
    normed = rms_normalize(full_rows, ffn_gain)
    pre_active = jnp.dot(
        normed,
        lax.all_gather(ffn_in, "grp", axis=0, tiled=True),
        preferred_element_type=jnp.float32,
    )
    hidden = jnp.maximum(pre_active, 0.0).astype(jnp.bfloat16)
    ffn_terms = jnp.dot(
        hidden,
        lax.all_gather(ffn_out, "grp", axis=1, tiled=True),
        preferred_element_type=jnp.float32,
    )
    ffn_sum = lax.psum_scatter(ffn_terms, "mdl", scatter_dimension=1, tiled=True)
    enc_state = (row_states.astype(jnp.float32) + ffn_sum).astype(jnp.bfloat16)
    capacity, send_rows, send_valid, got_valid = bucket_plan(
        row_question, rows_local, groups, my_group
    )
    head_cols = kv_weight.shape[2]
    outgoing = pack_slots(enc_state, send_rows, send_valid)
    arrived = lax.all_to_all(outgoing, "grp", split_axis=0, concat_axis=0, tiled=True)
    slot_rows = lax.all_gather(arrived.reshape(groups * capacity, -1), "mdl", axis=1, tiled=True)
    encoded = rms_normalize(slot_rows, final_gain)
    projected = jnp.einsum(
        "rd,kdc->krc", encoded, kv_weight, preferred_element_type=jnp.float32
    ).astype(jnp.bfloat16)
    key_rows = projected[0]
    value_rows = projected[1]
    targets = queries.shape[0]
    heads_local = head_cols // HEAD_DIM
    query_heads = queries.reshape(targets, heads_local, HEAD_DIM)
    key_heads = key_rows.reshape(-1, heads_local, HEAD_DIM)
    value_heads = value_rows.reshape(-1, heads_local, HEAD_DIM)
    scores = jnp.einsum("thd,rhd->htr", query_heads, key_heads, preferred_element_type=jnp.float32)
    slot_mask = got_valid[None, None, :]
    scores = jnp.where(slot_mask, scores, -1e30)
    top_score = jnp.max(scores, axis=-1, keepdims=True)
    raised = jnp.where(slot_mask, jnp.exp(scores - top_score), 0.0)
    probabilities = (raised / jnp.sum(raised, axis=-1, keepdims=True)).astype(jnp.bfloat16)
    attended = jnp.einsum(
        "htr,rhd->thd", probabilities, value_heads, preferred_element_type=jnp.float32
    )
    attended = attended.astype(jnp.bfloat16).reshape(targets, head_cols)
    return lax.psum_scatter(
        jnp.dot(attended, attn_out, preferred_element_type=jnp.float32).astype(jnp.bfloat16),
        "mdl",
        scatter_dimension=0,
        tiled=True,
    )


def solution(mesh):
    in_specs = (
        P("grp", "mdl"),
        P(),
        P("grp", "mdl"),
        P("mdl", "grp"),
        P(),
        P(None, None, "mdl"),
        P("grp", "mdl"),
        P("mdl", None),
        P(),
    )
    out_specs = P(("grp", "mdl"), None)
    return jax.shard_map(local, mesh=mesh, in_specs=in_specs, out_specs=out_specs, check_vma=False)
```

profile of v0, /device:TPU:8, one launch (start us, length us, event | category | flops | bytes accessed | tf_op | source)
XLA Modules:
  0.0 669.9 jit_solution(2616351746955564816)
XLA Ops:
  6.5 0.7 all-gather.4.cloned.1.call-update
  7.3 0.0 all-gather.6.cloned.1.call-start
  7.3 0.7 all-gather.6.cloned.1.call-update
  8.0 0.0 reduce-scatter.3.cloned.1.call-start
  8.1 0.7 convert_element_type.51
  8.7 56.0 %all_gather.12 = bf16[384,1024]{0,1:T(8,128)(2,1)S(1)} all-gather(bf16[384,32]{0,1:T(8,128)(2,1)} %param.9), channel_id=1, replica_groups=mesh['grp'=16,'mdl'=32] {'mdl'}, dimensions={1}, use_global_device_ids=true | all-gather | bytes 811008 | tf_op jit(solution)/shard_map/all_gather | solution.py:46
  64.7 0.2 fusion.14
  64.9 0.0 all-gather.4.cloned.1.call-done
  65.0 33.6 %all-gather.6.cloned.1.call-done = bf16[1024,1024]{0,1:T(8,128)(2,1)} async-done(((bf16[1024,64]{0,1:T(8,128)(2,1)}), bf16[1024,1024]{0,1:T(8,128)(2,1)}) %all-gather.6.cloned.1.call-update) | async-done | bytes 2097168 | tf_op jit(solution)/shard_map/all_gather | solution.py:56
  98.5 5.6 fusion.22
  104.1 0.0 reduce-scatter.3.cloned.1.call-update
  104.1 0.0 all-gather.8.cloned.1.call-start
  104.2 0.4 convert_reduce_fusion
  104.6 0.2 reduce_window_sum.11
  104.8 0.1 add_minimum_fusion
  104.8 0.1 min.22
  104.9 0.1 iota_compare_fusion.2
  105.0 0.2 broadcast_in_dim.60
  105.2 0.2 broadcast_in_dim.61
  105.5 0.2 broadcast_in_dim.62
  105.7 0.2 broadcast_in_dim.63
  106.0 222.1 %reduce-scatter.3.cloned.1.call-done = f32[384,32]{0,1:T(8,128)} async-done(((f32[384,1024]{0,1:T(8,128)}), f32[384,32]{0,1:T(8,128)}) %reduce-scatter.3.cloned.1.call-update) | async-done | bytes 49168 | tf_op jit(solution)/shard_map/reduce_scatter | solution.py:59
  328.1 0.8 add_convert_fusion
  328.9 0.1 copy.28
  329.0 2.9 gather_fusion
  332.0 0.2 gather.7
  332.2 0.5 broadcast.116
  332.7 0.7 reduce.5
  333.4 13.6 %all_to_all.6 = bf16[16,2,1152]{2,1,0:T(2,128)(2,1)S(1)} all-to-all(bf16[16,2,1152]{2,1,0:T(2,128)(2,1)S(1)} %reshape.169), channel_id=1, replica_groups=mesh['grp'=16,'mdl'=32] {'grp'}, dimensions={0} | all-to-all | bytes 147456 | tf_op jit(solution)/shard_map/all_to_all | solution.py:66
  347.0 0.1 reshape.170
  347.0 0.4 reduce.1
  347.5 0.2 reshape.154
  347.7 0.8 copy.30
  348.5 0.0 all-gather.8.cloned.1.call-update
  348.5 0.0 reduce-scatter.5.cloned.1.call-start
  348.6 0.2 dynamic-slice_reduce_fusion
  348.7 0.1 iota_compare_fusion.1
  348.8 0.1 lt.86
  348.9 78.2 %all-gather.8.cloned.1.call-done = bf16[1152,1024]{0,1:T(8,128)(2,1)} async-done(((bf16[1152,32]{0,1:T(8,128)(2,1)}), bf16[1152,1024]{0,1:T(8,128)(2,1)}) %all-gather.8.cloned.1.call-update) | async-done | bytes 2359312 | tf_op jit(solution)/shard_map/all_gather | solution.py:67
  427.1 2.3 fusion.2
  429.4 0.0 copy-done.1
  429.5 3.5 fusion.8
  432.9 1.2 fusion.40
  434.2 5.5 fusion.41
  439.7 2.9 fusion.17
  442.6 1.3 convolution_convert_fusion.1
  443.9 0.0 reduce-scatter.5.cloned.1.call-update
  443.9 219.4 %reduce-scatter.5.cloned.1.call-done = bf16[8,1024]{1,0:T(8,128)(2,1)} async-done(((bf16[256,1024]{1,0:T(8,128)(2,1)}), bf16[8,1024]{1,0:T(8,128)(2,1)}) %reduce-scatter.5.cloned.1.call-update) | async-done | bytes 16400 | tf_op jit(solution)/shard_map/reduce_scatter | solution.py:89
  (23 shorter events, 0.1 us)
Async XLA Ops:
  6.5 422.9 %copy-start = (bf16[2,1024,512]{2,1,0:T(8,128)(2,1)S(1)}, bf16[2,1024,512]{2,1,0:T(8,128)(2,1)}, u32[]{:S(2)}) copy-start(bf16[2,1024,512]{2,1,0:T(8,128)(2,1)} %param.14) | copy-start | bytes 6291460
  6.5 58.4 %all-gather.4.cloned.1.call-start = ((), (), s32[]{:S(2)}) async-start(), calls=%async_computation.3 | async-start | bytes 2228224 | tf_op jit(solution)/shard_map/all_gather | solution.py:50
  7.3 91.3 %all-gather.6.cloned.1.call-start = ((), (), s32[]{:S(2)}) async-start(), calls=%async_computation.4 | async-start | bytes 2228224 | tf_op jit(solution)/shard_map/all_gather | solution.py:56
  8.0 320.1 %reduce-scatter.3.cloned.1.call-start = ((), (), s32[]{:S(2)}) async-start(), calls=%async_computation.5 | async-start | bytes 1622016 | tf_op jit(solution)/shard_map/reduce_scatter | solution.py:59
  64.9 39.3 %copy-start.4 = (s32[6144]{0:T(1024)S(1)}, s32[6144]{0:T(1024)}, u32[]{:S(2)}) copy-start(s32[6144]{0:T(1024)} %param.17) | copy-start | bytes 73732
  104.1 224.0 %copy-start.3 = (bf16[384,32]{0,1:T(8,128)(2,1)S(1)}, bf16[384,32]{0,1:T(8,128)(2,1)}, u32[]{:S(2)}) copy-start(bf16[384,32]{0,1:T(8,128)(2,1)} %param.9) | copy-start | bytes 73732
  104.1 322.9 %all-gather.8.cloned.1.call-start = ((), (), s32[]{:S(2)}) async-start(), calls=%async_computation.6 | async-start | bytes 2433024 | tf_op jit(solution)/shard_map/all_gather | solution.py:67
  329.0 19.5 %copy-start.5 = (bf16[1024]{0:T(1024)(128)(2,1)S(1)}, bf16[1024]{0:T(1024)(128)(2,1)}, u32[]{:S(2)}) copy-start(bf16[1024]{0:T(1024)(128)(2,1)} %param.13) | copy-start | bytes 6148
  348.5 314.8 %reduce-scatter.5.cloned.1.call-start = ((), (), s32[]{:S(2)}) async-start(), calls=%async_computation.7 | async-start | bytes 540672 | tf_op jit(solution)/shard_map/reduce_scatter | solution.py:89
  427.1 2.4 copy-start.1
  432.9 1.2 copy-start.6
  439.7 3.0 copy-start.2
Sparse Core Ops, SparseCore 0:
  9.5 46.1 all-gather.3
  57.7 40.7 all-gather.5
  104.3 223.7 reduce-scatter.2
  348.6 78.4 all-gather.7
  444.0 219.2 reduce-scatter.4
where the time goes:
time: 670 us
  waiting for transfers between devices  555 us (83%)
  blocking collectives  69.5 us (10%)
  matrix products  18.7 us (3%)
  between operations  13.3 us (2%)
  local copies, waits for them, and re-layouts  7.41 us (1%)
    reduce_scatter x1, waiting for transfers between devices, local(): lax.psum_scatter(ffn_terms, 'mdl', scatter_dimension=1, tiled=True)  222 us
    reduce_scatter x1, waiting for transfers between devices, local(): lax.psum_scatter(jnp.dot(attended, attn_out, preferred_element_type=jnp.f...  219 us
    all_gather x1, waiting for transfers between devices, local(): lax.all_gather(arrived.reshape(groups * capacity, -1), 'mdl', axis=1, til...  78.2 us
    all_gather x1, blocking collectives, local(): full_rows = lax.all_gather(row_states, 'mdl', axis=1, tiled=True)  56 us
    all_gather x1, waiting for transfers between devices, local(): lax.all_gather(ffn_out, 'grp', axis=1, tiled=True)  33.6 us
    all_to_all x1, blocking collectives, local(): lax.all_to_all(outgoing, 'grp', split_axis=0, concat_axis=0, tiled=True)  13.6 us
  transfers between devices with their start and end apart: 5, of which 4 were waited for; matrix products, arithmetic and copies ran while one was open for 0% of the time, Pallas kernels for 0%

commit v1 on v0

--- a/solution.py
+++ b/solution.py
@@ -43,7 +43,9 @@
     groups = lax.axis_size("grp")
     my_group = lax.axis_index("grp")
     rows_local = row_states.shape[0]
-    full_rows = lax.all_gather(row_states, "mdl", axis=1, tiled=True)
+    full_rows = jnp.concatenate(
+        lax.all_to_all(jnp.stack([row_states] * lax.axis_size("mdl")), "mdl", 0, 0), axis=1
+    )
     normed = rms_normalize(full_rows, ffn_gain)
     pre_active = jnp.dot(
         normed,

time: 670 us -> 670 us (level)
  blocking collectives: 69.5 us -> 13.6 us
  waiting for transfers between devices: 555 us -> 595 us
  starting transfers between devices: 0.16 us -> 13.3 us
    all_gather x1 -> x0, blocking collectives: 56 us -> none  [local(): full_rows = lax.all_gather(row_states, 'mdl', axis=1, tiled=True)]
    all_to_all x0 -> x1, waiting for transfers between devices: none -> 23.3 us  [local(): lax.all_to_all(jnp.stack([row_states] * lax.axis_size('mdl')), 'mdl', 0, 0)]
    all_to_all x0 -> x1, starting transfers between devices: none -> 13.2 us  [local(): lax.all_to_all(jnp.stack([row_states] * lax.axis_size('mdl')), 'mdl', 0, 0)]
    all_gather x1, waiting for transfers between devices: 33.6 us -> 43 us  [local(): lax.all_gather(ffn_out, 'grp', axis=1, tiled=True)]
    all_gather x1, waiting for transfers between devices: 0.02 us -> 7.94 us  [local(): lax.all_gather(ffn_in, 'grp', axis=0, tiled=True)]
  transfers between devices with their start and end apart: 5 -> 6, of which waited for: 4 -> 6; matrix products, arithmetic and copies ran while one was open for 0% -> 1% of each run, Pallas kernels for 0% -> 0%
where the time goes in v1:
time: 670 us
  waiting for transfers between devices  595 us (89%)
  matrix products  18.9 us (3%)
  blocking collectives  13.6 us (2%)
  starting transfers between devices  13.3 us (2%)
  between operations  13.3 us (2%)
  local copies, waits for them, and re-layouts  9.1 us (1%)
    reduce_scatter x1, waiting for transfers between devices, local(): lax.psum_scatter(ffn_terms, 'mdl', scatter_dimension=1, tiled=True)  222 us
    reduce_scatter x1, waiting for transfers between devices, local(): lax.psum_scatter(jnp.dot(attended, attn_out, preferred_element_type=jnp.f...  219 us
    all_gather x1, waiting for transfers between devices, local(): lax.all_gather(arrived.reshape(groups * capacity, -1), 'mdl', axis=1, til...  78.1 us
    all_gather x1, waiting for transfers between devices, local(): lax.all_gather(ffn_out, 'grp', axis=1, tiled=True)  43 us
    all_to_all x1, waiting for transfers between devices, local(): lax.all_to_all(jnp.stack([row_states] * lax.axis_size('mdl')), 'mdl', 0, 0)  23.3 us
    all_to_all x1, blocking collectives, local(): lax.all_to_all(outgoing, 'grp', split_axis=0, concat_axis=0, tiled=True)  13.6 us
  transfers between devices with their start and end apart: 6, of which 6 were waited for; matrix products, arithmetic and copies ran while one was open for 1% of the time, Pallas kernels for 0%

profile of v1, /device:TPU:8, one launch (start us, length us, event | category | flops | bytes accessed | tf_op | source)
XLA Modules:
  0.0 669.8 jit_solution(13014033615071384939)
XLA Ops:
  6.5 0.7 all-gather.4.cloned.1.call-update
  7.3 0.0 all-gather.6.cloned.1.call-start
  7.3 0.7 all-gather.6.cloned.1.call-update
  8.0 1.7 stack.2
  9.7 13.2 %all-to-all-start = ((bf16[32,384,32]{1,2,0:T(8,128)(2,1)}), bf16[32,384,32]{1,2,0:T(8,128)(2,1)S(1)}, u32[]{:S(2)}, u32[]{:S(2)}) async-start(bf16[32,384,32]{1,2,0:T(8,128)(2,1)} %stack.2), calls=%async_computation | async-start | bytes 1572864 | tf_op jit(solution)/shard_map/all_to_all | solution.py:47
  22.9 0.0 reduce-scatter.3.cloned.1.call-start
  22.9 23.3 %all-to-all-done = bf16[32,384,32]{1,2,0:T(8,128)(2,1)S(1)} async-done(((bf16[32,384,32]{1,2,0:T(8,128)(2,1)}), bf16[32,384,32]{1,2,0:T(8,128)(2,1)S(1)}, u32[]{:S(2)}, u32[]{:S(2)}) %all-to-all-start) | async-done | bytes 786464 | tf_op jit(solution)/shard_map/all_to_all | solution.py:47
  46.2 0.2 multiply_reduce_fusion
  46.5 1.1 fusion.15
  47.6 7.9 %all-gather.4.cloned.1.call-done = bf16[1024,1024]{1,0:T(8,128)(2,1)} async-done(((bf16[64,1024]{1,0:T(8,128)(2,1)}), bf16[1024,1024]{1,0:T(8,128)(2,1)}) %all-gather.4.cloned.1.call-update) | async-done | bytes 2097168 | tf_op jit(solution)/shard_map/all_gather | solution.py:52
  55.5 43.0 %all-gather.6.cloned.1.call-done = bf16[1024,1024]{0,1:T(8,128)(2,1)} async-done(((bf16[1024,64]{0,1:T(8,128)(2,1)}), bf16[1024,1024]{0,1:T(8,128)(2,1)}) %all-gather.6.cloned.1.call-update) | async-done | bytes 2097168 | tf_op jit(solution)/shard_map/all_gather | solution.py:58
  98.5 5.7 fusion.17
  104.3 0.0 reduce-scatter.3.cloned.1.call-update
  104.3 0.0 all-gather.8.cloned.1.call-start
  104.4 0.4 convert_reduce_fusion
  104.7 0.2 reduce_window_sum.11
  104.9 0.1 add_minimum_fusion
  105.0 0.1 min.22
  105.1 0.1 iota_compare_fusion.2
  105.2 0.2 broadcast_in_dim.60
  105.4 0.2 broadcast_in_dim.61
  105.6 0.2 broadcast_in_dim.62
  105.9 0.2 broadcast_in_dim.63
  106.1 222.2 %reduce-scatter.3.cloned.1.call-done = f32[384,32]{0,1:T(8,128)} async-done(((f32[384,1024]{0,1:T(8,128)}), f32[384,32]{0,1:T(8,128)}) %reduce-scatter.3.cloned.1.call-update) | async-done | bytes 49168 | tf_op jit(solution)/shard_map/reduce_scatter | solution.py:61
  328.3 0.8 add_convert_fusion
  329.1 0.1 copy.29
  329.2 2.9 gather_fusion
  332.2 0.2 gather.7
  332.4 0.5 broadcast.118
  332.9 0.7 reduce.7
  333.6 13.6 %all_to_all.11 = bf16[16,2,1152]{2,1,0:T(2,128)(2,1)S(1)} all-to-all(bf16[16,2,1152]{2,1,0:T(2,128)(2,1)S(1)} %reshape.176), channel_id=1, replica_groups=mesh['grp'=16,'mdl'=32] {'grp'}, dimensions={0} | all-to-all | bytes 147456 | tf_op jit(solution)/shard_map/all_to_all | solution.py:68
  347.2 0.1 reshape.177
  347.2 0.4 reduce.3
  347.7 0.2 reshape.160
  347.9 0.8 copy.31
  348.7 0.0 all-gather.8.cloned.1.call-update
  348.7 0.0 reduce-scatter.5.cloned.1.call-start
  348.8 0.2 dynamic-slice_reduce_fusion
  348.9 0.1 iota_compare_fusion.1
  349.0 0.1 lt.86
  349.1 78.1 %all-gather.8.cloned.1.call-done = bf16[1152,1024]{0,1:T(8,128)(2,1)} async-done(((bf16[1152,32]{0,1:T(8,128)(2,1)}), bf16[1152,1024]{0,1:T(8,128)(2,1)}) %all-gather.8.cloned.1.call-update) | async-done | bytes 2359312 | tf_op jit(solution)/shard_map/all_gather | solution.py:69
  427.3 2.3 fusion.2
  429.7 3.5 fusion.8
  433.1 1.2 fusion.34
  434.4 5.5 fusion.35
  439.8 3.0 fusion.16
  442.8 1.3 convolution_convert_fusion.1
  444.1 219.2 %reduce-scatter.5.cloned.1.call-done = bf16[8,1024]{1,0:T(8,128)(2,1)} async-done(((bf16[256,1024]{1,0:T(8,128)(2,1)}), bf16[8,1024]{1,0:T(8,128)(2,1)}) %reduce-scatter.5.cloned.1.call-update) | async-done | bytes 16400 | tf_op jit(solution)/shard_map/reduce_scatter | solution.py:91
  (28 shorter events, 0.2 us)
Async XLA Ops:
  6.5 423.1 %copy-start = (bf16[2,1024,512]{2,1,0:T(8,128)(2,1)S(1)}, bf16[2,1024,512]{2,1,0:T(8,128)(2,1)}, u32[]{:S(2)}) copy-start(bf16[2,1024,512]{2,1,0:T(8,128)(2,1)} %param.14) | copy-start | bytes 6291460
  6.5 16.4 %copy-start.5 = (bf16[1024]{0:T(1024)(128)(2,1)S(1)}, bf16[1024]{0:T(1024)(128)(2,1)}, u32[]{:S(2)}) copy-start(bf16[1024]{0:T(1024)(128)(2,1)} %param.10) | copy-start | bytes 6148
  6.5 49.0 %all-gather.4.cloned.1.call-start = ((), (), s32[]{:S(2)}) async-start(), calls=%async_computation.4 | async-start | bytes 2228224 | tf_op jit(solution)/shard_map/all_gather | solution.py:52
  7.3 91.3 %all-gather.6.cloned.1.call-start = ((), (), s32[]{:S(2)}) async-start(), calls=%async_computation.5 | async-start | bytes 2228224 | tf_op jit(solution)/shard_map/all_gather | solution.py:58
  9.7 36.5 %all-to-all-start = ((bf16[32,384,32]{1,2,0:T(8,128)(2,1)}), bf16[32,384,32]{1,2,0:T(8,128)(2,1)S(1)}, u32[]{:S(2)}, u32[]{:S(2)}) async-start(bf16[32,384,32]{1,2,0:T(8,128)(2,1)} %stack.2), calls=%async_computation | async-start | bytes 1572864 | tf_op jit(solution)/shard_map/all_to_all | solution.py:47
  22.9 305.4 %reduce-scatter.3.cloned.1.call-start = ((), (), s32[]{:S(2)}) async-start(), calls=%async_computation.6 | async-start | bytes 1622016 | tf_op jit(solution)/shard_map/reduce_scatter | solution.py:61
  47.6 56.8 %copy-start.4 = (s32[6144]{0:T(1024)S(1)}, s32[6144]{0:T(1024)}, u32[]{:S(2)}) copy-start(s32[6144]{0:T(1024)} %param.17) | copy-start | bytes 73732
  104.3 224.0 %copy-start.3 = (bf16[384,32]{0,1:T(8,128)(2,1)S(1)}, bf16[384,32]{0,1:T(8,128)(2,1)}, u32[]{:S(2)}) copy-start(bf16[384,32]{0,1:T(8,128)(2,1)} %param.9) | copy-start | bytes 73732
  104.3 323.0 %all-gather.8.cloned.1.call-start = ((), (), s32[]{:S(2)}) async-start(), calls=%async_computation.7 | async-start | bytes 2433024 | tf_op jit(solution)/shard_map/all_gather | solution.py:69
  329.2 19.5 %copy-start.6 = (bf16[1024]{0:T(1024)(128)(2,1)S(1)}, bf16[1024]{0:T(1024)(128)(2,1)}, u32[]{:S(2)}) copy-start(bf16[1024]{0:T(1024)(128)(2,1)} %param.13) | copy-start | bytes 6148
  348.7 314.6 %reduce-scatter.5.cloned.1.call-start = ((), (), s32[]{:S(2)}) async-start(), calls=%async_computation.8 | async-start | bytes 540672 | tf_op jit(solution)/shard_map/reduce_scatter | solution.py:91
  427.3 2.4 copy-start.1
  433.1 1.2 copy-start.7
  439.8 3.0 copy-start.2
Sparse Core Ops, SparseCore 0:
  9.5 46.0 all-gather.3
  57.6 40.8 all-gather.5
  104.4 223.8 reduce-scatter.2
  348.8 78.4 all-gather.7
  444.2 218.9 reduce-scatter.4
